TPU v7x, 32 devices: a whole 2x2x4 slice. The times are simulated.
32 devices in a mesh: leaf: 4 (over x, core), blk: 8 (over z, y).
Axes of the slice: x: 2, y: 2, z: 4, core: 2. Of those that a mesh axis runs over, the one named last changes fastest.
Arguments:
- right_side: float32 [4, 8, 448, 128], P('leaf', 'blk'), may hold values from -6 to 6
- inverse_blocks: bfloat16 [4, 8, 448, 2048], P('leaf', 'blk'), may hold values from -0.125 to 0.125
- coupling: bfloat16 [4, 8, 640, 1024], P('leaf', 'blk'), may hold values from -0.0625 to 0.0625
- update_rows: int32 [10, 1024], replicated, may hold values from 0 to 2047, as said below
Outputs:
- solution: float32 [4, 8, 448, 128], P('leaf', 'blk')
Inputs may be any that keep to these rules, and one draw needn't show every extreme that they name: `update_rows`: the 1024 entries of each row are distinct.
All inputs are finite; a program needn't handle non-finite values.
Results may differ from a plain program's by a relative error of at most 0.0075.
Values may be sent and summed in bfloat16 or wider, within the bound.
No kernel may reach another device: no remote copies, remote signals or barrier semaphores. Data moves between devices by JAX's collectives and lax.ppermute only.
A program may use at most 64 MiB of HBM per device.

v0:
```python
import jax
import jax.numpy as jnp
from jax import lax
from jax.sharding import PartitionSpec as P


def from_partner(shard, axis, distance):
    return lax.ppermute(shard, axis, [(i, i ^ 1 << distance) for i in range(lax.axis_size(axis))])


def group_total(partial_value, level_no, leaf_id, want_full):
    members = partial_value.shape[0]
    member = leaf_id & members - 1
    full_rows = None
    summed = lax.psum_scatter(partial_value, "blk", scatter_dimension=1, tiled=True)
    for bit_no in range(level_no):
        summed = summed + from_partner(summed, "leaf", bit_no)
    own_rows = lax.dynamic_index_in_dim(summed, member, 0, keepdims=False)[0]
    if want_full:
        full_rows = lax.all_gather(summed.astype(jnp.bfloat16), "blk", axis=1, tiled=True)
    if full_rows is not None:
        full_rows = full_rows.reshape(-1, full_rows.shape[-1])
    return (own_rows, full_rows)


def local(right_side, inverse_blocks, coupling, update_rows):
    leaves = lax.axis_size("leaf")
    blocks = lax.axis_size("blk")
    tree_depth = leaves.bit_length() - 1
    leaf_id = lax.axis_index("leaf")
    blk_id = lax.axis_index("blk")
    node_width = inverse_blocks.shape[-1]
    load_cases = right_side.shape[-1]
    local_rhs = right_side[0, 0]
    local_inverse = inverse_blocks[0, 0]
    local_coupling = coupling[0, 0]
    row_counts = [node_width // (blocks << level_no) for level_no in range(tree_depth + 1)]
    row_starts = [sum(row_counts[:level_no]) for level_no in range(tree_depth + 1)]
    coupling_starts = {}
    cursor = 0
    for level_no in range(tree_depth):
        for ancestor in range(level_no + 1, tree_depth + 1):
            coupling_starts[level_no, ancestor] = cursor
            cursor += row_counts[level_no]
    pair_bases = []
    cursor = 0
    for level_no in range(tree_depth + 1):
        pair_bases.append(cursor)
        cursor += (leaves >> level_no) * (tree_depth - level_no)

    def coupling_block(level_no, ancestor):
        coup_start = coupling_starts[level_no, ancestor]
        return local_coupling[coup_start : coup_start + row_counts[level_no]]

    def row_list(level_no, ancestor):
        node_id = leaf_id >> level_no
        pair_row = (
            pair_bases[level_no] + node_id * (tree_depth - level_no) + (ancestor - level_no - 1)
        )
        return lax.dynamic_index_in_dim(update_rows, pair_row, 0, keepdims=False)

    pending = {}
    y_levels = []
    for level_no in range(tree_depth + 1):
        members = 1 << level_no
        row_count = row_counts[level_no]
        row_start = row_starts[level_no]
        member = leaf_id & members - 1
        if level_no == 0:
            residual = lax.all_gather(
                local_rhs[row_start : row_start + row_count].astype(jnp.bfloat16),
                "blk",
                axis=0,
                tiled=True,
            )
        else:
            buffer = pending.get(level_no, jnp.zeros((node_width, load_cases), jnp.float32))
            slot_start = (member * blocks + blk_id) * row_count
            current = lax.dynamic_slice_in_dim(buffer, slot_start, row_count, 0)
            buffer = lax.dynamic_update_slice_in_dim(
                buffer, current + local_rhs[row_start : row_start + row_count], slot_start, 0
            )
            unused_rows, residual = group_total(
                buffer.reshape(members, blocks, row_count, load_cases), level_no, leaf_id, True
            )
        inverse_rows = local_inverse[row_start : row_start + row_count]
        y_rows = jnp.dot(inverse_rows, residual, preferred_element_type=jnp.float32)
        y_levels.append(y_rows)
        y_round = y_rows.astype(jnp.bfloat16)
        for ancestor in range(level_no + 1, tree_depth + 1):
            contrib = lax.dot_general(
                coupling_block(level_no, ancestor),
                y_round,
                (((0,), (0,)), ((), ())),
                preferred_element_type=jnp.float32,
            )
            summed = pending.get(ancestor, jnp.zeros((node_width, load_cases), jnp.float32))
            pending[ancestor] = summed.at[row_list(level_no, ancestor)].add(-contrib)
    solved = {}
    outputs = [None] * (tree_depth + 1)
    for level_no in range(tree_depth, -1, -1):
        members = 1 << level_no
        row_count = row_counts[level_no]
        row_start = row_starts[level_no]
        z_rows = y_levels[level_no]
        for ancestor in range(level_no + 1, tree_depth + 1):
            picked = jnp.take(solved[ancestor], row_list(level_no, ancestor), axis=0)
            z_rows = z_rows - jnp.dot(
                coupling_block(level_no, ancestor), picked, preferred_element_type=jnp.float32
            )
        inverse_rows = local_inverse[row_start : row_start + row_count]
        partial_value = lax.dot_general(
            inverse_rows,
            z_rows.astype(jnp.bfloat16),
            (((0,), (0,)), ((), ())),
            preferred_element_type=jnp.float32,
        )
        own_rows, full_rows = group_total(
            partial_value.reshape(members, blocks, row_count, load_cases),
            level_no,
            leaf_id,
            level_no > 0,
        )
        outputs[level_no] = own_rows
        if level_no > 0:
            solved[level_no] = full_rows
    return jnp.concatenate(outputs, 0)[None, None]


def solution(mesh):
    in_specs = (
        P("leaf", "blk", None, None),
        P("leaf", "blk", None, None),
        P("leaf", "blk", None, None),
        P(),
    )
    out_specs = P("leaf", "blk", None, None)
    return jax.shard_map(local, mesh=mesh, in_specs=in_specs, out_specs=out_specs, check_vma=False)
```

profile of v0, /device:TPU:0, one launch (start us, length us, event | category | flops | bytes accessed | tf_op | source)
XLA Modules:
  0.0 612.2 jit_solution(16145240339841454955)
XLA Ops:
  6.5 1.0 slice.135
  7.6 33.0 %all-gather = bf16[1,1,2048,128]{3,2,1,0:T(8,128)(2,1)S(1)} all-gather(bf16[1,1,256,128]{3,2,1,0:T(8,128)(2,1)S(1)} %slice.135), channel_id=2, replica_groups=mesh['leaf'=4,'blk'=8] {'blk'}, dimensions={2}, use_global_device_ids=true | all-gather | bytes 589824 | tf_op jit(solution)/shard_map/all_gather | solution.py:70
  40.6 1.6 fusion.8
  42.2 0.3 fusion.2
  42.7 1.4 compare_select_fusion.2
  44.2 6.3 %scatter_custom_fusion = f32[2048,128]{1,0:T(8,128)S(1)} fusion(s32[1024]{0:T(1024)S(1)} %bitcast.138, f32[1024,128]{1,0:T(8,128)S(1)} %copy.20, f32[]{:T(128)} %constant.56.clone.1), kind=kCustom, calls=%fused_computation.38 | custom fusion | flops 131072 | bytes 1048580 | tf_op jit(solution)/shard_map/scatter-add | solution.py:98
  50.4 0.9 fusion.57
  51.3 1.0 copy-done.1
  52.4 0.7 dynamic-slice
  53.1 78.9 %all-reduce.7.cloned.1.call-done = f32[2,8,128,128]{3,2,1,0:T(8,128)} async-done(((f32[2,8,128,128]{3,2,1,0:T(8,128)}), f32[2,8,128,128]{3,2,1,0:T(8,128)}) %all-reduce.7.cloned.1.call-update) | async-done | bytes 1048592
  132.0 2.2 constant_dynamic-slice_fusion.5
  134.7 6.5 %scatter_custom_fusion.1 = f32[2048,128]{1,0:T(8,128)S(1)} fusion(s32[1024]{0:T(1024)} %bitcast.137, f32[1024,128]{1,0:T(8,128)S(1)} %copy.21, f32[]{:T(128)} %constant.56.clone.1), kind=kCustom, calls=%fused_computation.36 | custom fusion | flops 131072 | bytes 1049088 | tf_op jit(solution)/shard_map/scatter-add | solution.py:98
  141.3 1.6 add_convert_fusion.1
  142.9 31.4 %all_gather.16 = bf16[2,8,128,128]{3,2,1,0:T(8,128)(2,1)S(1)} all-gather(bf16[2,1,128,128]{3,2,1,0:T(8,128)(2,1)S(1)} %add_convert_fusion.1), channel_id=1, replica_groups=mesh['leaf'=4,'blk'=8] {'blk'}, dimensions={1}, use_global_device_ids=true | all-gather | bytes 589824 | tf_op jit(solution)/shard_map/all_gather | solution.py:20
  174.3 0.3 fusion.16
  174.6 2.0 fusion
  176.6 1.2 copy.22
  177.8 6.4 %scatter_fusion = f32[2048,128]{1,0:T(8,128)S(1)} fusion(f32[2048,128]{1,0:T(8,128)S(1)} %scatter_custom_fusion.1, s32[1024]{0:T(1024)S(1)} %bitcast.136, f32[1024,128]{1,0:T(8,128)S(1)} %copy.22), kind=kCustom, calls=%fused_computation.5 | custom fusion | flops 131072 | bytes 1576960 | tf_op jit(solution)/shard_map/scatter-add | solution.py:98
  184.3 0.8 fusion.58
  185.0 1.0 copy-done
  186.1 77.9 %all-reduce.9.cloned.1.call-done = f32[4,8,64,128]{3,2,1,0:T(8,128)} async-done(((f32[4,8,64,128]{3,2,1,0:T(8,128)}), f32[4,8,64,128]{3,2,1,0:T(8,128)}) %all-reduce.9.cloned.1.call-update) | async-done | bytes 1048592
  264.0 1.6 constant_dynamic-slice_fusion.4
  265.7 1.3 collective-permute-done.1
  267.0 1.6 fusion.75
  268.6 1.5 collective-permute-start.2
  270.1 4.1 collective-permute-done.2
  274.2 31.3 %all_gather.17 = bf16[4,8,64,128]{3,2,1,0:T(8,128)(2,1)S(1)} all-gather(bf16[4,1,64,128]{3,2,1,0:T(8,128)(2,1)S(1)} %add_convert_fusion), channel_id=1, replica_groups=mesh['leaf'=4,'blk'=8] {'blk'}, dimensions={1}, use_global_device_ids=true | all-gather | bytes 589824 | tf_op jit(solution)/shard_map/all_gather | solution.py:20
  305.5 0.5 convolution_bitcast_fusion.1
  306.0 1.4 copy.23
  307.5 78.2 %all-reduce.11.cloned.1.call-done = f32[4,8,64,128]{3,2,1,0:T(8,128)} async-done(((f32[4,8,64,128]{3,2,1,0:T(8,128)}), f32[4,8,64,128]{3,2,1,0:T(8,128)}) %all-reduce.11.cloned.1.call-update) | async-done | bytes 1048592
  385.6 1.6 constant_dynamic-slice_fusion.3
  387.3 1.3 collective-permute-done.3
  388.6 1.6 fusion.74
  390.2 1.5 collective-permute-start.4
  391.8 4.1 collective-permute-done.4
  395.9 31.3 %all_gather.18 = bf16[4,8,64,128]{3,2,1,0:T(8,128)(2,1)S(1)} all-gather(bf16[4,1,64,128]{3,2,1,0:T(8,128)(2,1)S(1)} %get-tuple-element.8), channel_id=1, replica_groups=mesh['leaf'=4,'blk'=8] {'blk'}, dimensions={1}, use_global_device_ids=true | all-gather | bytes 589824 | tf_op jit(solution)/shard_map/all_gather | solution.py:20
  427.1 3.2 gather_fusion
  430.4 2.0 convolution_bitcast_fusion.2
  432.5 1.4 copy.24
  434.0 64.1 %reduce-scatter.12.cloned.1.call-done = f32[2,1,128,128]{3,2,0,1:T(8,128)} async-done(((f32[2,8,128,128]{3,2,0,1:T(8,128)}), f32[2,1,128,128]{3,2,0,1:T(8,128)}) %reduce-scatter.12.cloned.1.call-update) | async-done | bytes 131088 | tf_op jit(solution)/shard_map/reduce_scatter | solution.py:15
  498.1 3.2 gather_fusion.2
  501.4 31.5 %all_gather.19 = bf16[2,8,128,128]{3,2,0,1:T(8,128)(2,1)S(1)} all-gather(bf16[2,1,128,128]{3,2,0,1:T(8,128)(2,1)S(1)} %get-tuple-element.6), channel_id=1, replica_groups=mesh['leaf'=4,'blk'=8] {'blk'}, dimensions={1}, use_global_device_ids=true | all-gather | bytes 589824 | tf_op jit(solution)/shard_map/all_gather | solution.py:20
  532.9 3.2 gather_fusion.1
  536.1 1.5 fusion.4
  537.6 1.8 convolution_bitcast_fusion
  539.4 1.3 copy.31
  540.8 63.3 %reduce-scatter.14.cloned.1.call-done = f32[1,1,256,128]{3,2,1,0:T(8,128)} async-done(((f32[1,8,256,128]{3,2,1,0:T(8,128)}), f32[1,1,256,128]{3,2,1,0:T(8,128)}) %reduce-scatter.14.cloned.1.call-update) | async-done | bytes 131088 | tf_op jit(solution)/shard_map/reduce_scatter | solution.py:15
  604.1 1.6 maximum_bitcast_fusion
  (47 shorter events, 1.4 us)
Async XLA Ops:
  6.5 125.5 %all-reduce.7.cloned.1.call-start = ((), (), s32[]{:S(2)}) async-start(), calls=%async_computation.4 | async-start | bytes 2097152
  6.5 35.7 %copy-start.4 = (bf16[1,1,640,1024]{3,2,1,0:T(8,128)(2,1)S(1)}, bf16[1,1,640,1024]{3,2,1,0:T(8,128)(2,1)}, u32[]{:S(2)}) copy-start(bf16[1,1,640,1024]{3,2,1,0:T(8,128)(2,1)} %param.8) | copy-start | bytes 3932164
  42.2 92.0 %copy-start.5 = (f32[256,128]{1,0:T(8,128)}, f32[256,128]{1,0:T(8,128)S(1)}, u32[]{:S(2)}) copy-start(f32[256,128]{1,0:T(8,128)S(1)} %fusion.8) | copy-start | bytes 393220
  42.7 9.7 %copy-start.8 = (u32[32]{0:T(128)S(1)}, u32[32]{0:T(128)}, u32[]{:S(2)}) copy-start(u32[32]{0:T(128)} %constant.76) | copy-start | bytes 388
  51.3 1.0 copy-start.1
  52.3 211.6 %all-reduce.9.cloned.1.call-start = ((), (), s32[]{:S(2)}) async-start(), calls=%async_computation.5 | async-start | bytes 2097152
  134.2 7.0 %collective-permute-start = (f32[2,1,128,128]{3,2,1,0:T(8,128)}, f32[2,1,128,128]{3,2,1,0:T(8,128)S(1)}, u32[]{:S(2)}, u32[]{:S(2)}) collective-permute-start(f32[2,1,128,128]{3,2,1,0:T(8,128)} %constant_dynamic-slice_fusion.5), channel_id=1, source_target_pairs={{0,8},{8,0},{16,24},{24,16},{1,9},{9,1},{17,25},{25,17},{2,10},{10... | collective-permute-start | bytes 393224 | tf_op jit(solution)/shard_map/ppermute | solution.py:8
  134.5 39.8 %copy-start.2 = (bf16[1,1,448,2048]{3,2,1,0:T(8,128)(2,1)S(1)}, bf16[1,1,448,2048]{3,2,1,0:T(8,128)(2,1)}, u32[]{:S(2)}) copy-start(bf16[1,1,448,2048]{3,2,1,0:T(8,128)(2,1)} %param.7) | copy-start | bytes 5505028
  185.0 1.0 copy-start
  186.1 199.6 %all-reduce.11.cloned.1.call-start = ((), (), s32[]{:S(2)}) async-start(), calls=%async_computation.6 | async-start | bytes 2097152
  265.6 1.4 collective-permute-start.1
  268.6 5.6 collective-permute-start.2
  307.4 190.7 %reduce-scatter.12.cloned.1.call-start = ((), (), s32[]{:S(2)}) async-start(), calls=%async_computation.2 | async-start | bytes 1179648 | tf_op jit(solution)/shard_map/reduce_scatter | solution.py:15
  387.2 1.4 collective-permute-start.3
  390.2 5.6 collective-permute-start.4
  434.0 170.1 %reduce-scatter.14.cloned.1.call-start = ((), (), s32[]{:S(2)}) async-start(), calls=%async_computation.3 | async-start | bytes 1179648 | tf_op jit(solution)/shard_map/reduce_scatter | solution.py:15
  498.1 3.2 copy-start.7
  498.1 3.2 collective-permute-start.5
  532.9 3.2 copy-start.6
  532.9 4.7 copy-start.3
Sparse Core Ops, SparseCore 0:
  52.5 79.4 all-reduce.6
  186.2 77.7 all-reduce.8
  307.5 78.0 all-reduce.10
  434.1 63.9 reduce-scatter.11
  540.9 63.1 reduce-scatter.13
where the time goes:
time: 613 us; the launch traced here: 612 us
  waiting for transfers between devices  373 us (61%)
  blocking collectives  158 us (26%)
  other arithmetic  28.8 us (5%)
  local copies, waits for them, and re-layouts  24.7 us (4%)
  between operations  13.5 us (2%)
  matrix products  10.2 us (2%)
    unnamed x8, waiting for transfers between devices  235 us
    reduce_scatter x2, waiting for transfers between devices, group_total(): lax.psum_scatter(partial_value, 'blk', scatter_dimension=1, tiled=True)  127 us
    all_gather x4, blocking collectives, group_total(): lax.all_gather(summed.astype(jnp.bfloat16), 'blk', axis=1, tiled=True)  125 us
    all_gather x1, blocking collectives, local(): lax.all_gather(local_rhs[row_start:row_start + row_count].astype(jnp.bflo...  33 us
    scatter-add x3, other arithmetic, local(): pending[ancestor] = summed.at[row_list(level_no, ancestor)].add(-contrib)  19.2 us
  transfers between devices with their start and end apart: 11, of which 9 were waited for; matrix products, arithmetic and copies ran while one was open for 2% of the time, Pallas kernels for 0%

commit v1 on v0

--- a/solution.py
+++ b/solution.py
@@ -17,7 +17,20 @@
         summed = summed + from_partner(summed, "leaf", bit_no)
     own_rows = lax.dynamic_index_in_dim(summed, member, 0, keepdims=False)[0]
     if want_full:
-        full_rows = lax.all_gather(summed.astype(jnp.bfloat16), "blk", axis=1, tiled=True)
+
+        def lane_shape(obj, comm_axis, at_axis):
+            cores_n = lax.axis_size(comm_axis)
+            kept_rows = list(map(lambda w: cores_n if w == at_axis else 1, range(obj.ndim)))
+            plain = lax.all_to_all(
+                jnp.tile(obj, kept_rows),
+                comm_axis,
+                split_axis=at_axis,
+                concat_axis=at_axis,
+                tiled=True,
+            )
+            return plain
+
+        full_rows = lane_shape(summed.astype(jnp.bfloat16), comm_axis="blk", at_axis=1)
     if full_rows is not None:
         full_rows = full_rows.reshape(-1, full_rows.shape[-1])
     return (own_rows, full_rows)

time: 613 us -> 555 us (0.905)
  blocking collectives: 158 us -> 51 us
  waiting for transfers between devices: 373 us -> 407 us
  starting transfers between devices: 3.38 us -> 15.5 us
    all_gather x4 -> x0, blocking collectives: 125 us -> none  [group_total(): lax.all_gather(summed.astype(jnp.bfloat16), 'blk', axis=1, tiled=True)]
    all_to_all x0 -> x3, waiting for transfers between devices: none -> 32.1 us  [lane_shape(): lax.all_to_all(jnp.tile(obj, kept_rows), comm_axis, split_axis=at_axis, c...]
    all_to_all x0 -> x1, blocking collectives: none -> 17.9 us  [lane_shape(): lax.all_to_all(jnp.tile(obj, kept_rows), comm_axis, split_axis=at_axis, c...]
    all_to_all x0 -> x3, starting transfers between devices: none -> 12 us  [lane_shape(): lax.all_to_all(jnp.tile(obj, kept_rows), comm_axis, split_axis=at_axis, c...]
  transfers between devices with their start and end apart: 11 -> 14, of which waited for: 9 -> 14; matrix products, arithmetic and copies ran while one was open for 2% -> 2% of each run, Pallas kernels for 0% -> 0%
where the time goes in v1:
time: 555 us; the launch traced here: 554 us
  waiting for transfers between devices  407 us (73%)
  blocking collectives  51 us (9%)
  other arithmetic  29.2 us (5%)
  local copies, waits for them, and re-layouts  27.5 us (5%)
  starting transfers between devices  15.5 us (3%)
  between operations  13.5 us (2%)
  matrix products  10.9 us (2%)
    unnamed x8, waiting for transfers between devices  234 us
    reduce_scatter x2, waiting for transfers between devices, group_total(): lax.psum_scatter(partial_value, 'blk', scatter_dimension=1, tiled=True)  127 us
    all_gather x1, blocking collectives, local(): lax.all_gather(local_rhs[row_start:row_start + row_count].astype(jnp.bflo...  33 us
    all_to_all x3, waiting for transfers between devices, lane_shape(): lax.all_to_all(jnp.tile(obj, kept_rows), comm_axis, split_axis=at_axis, c...  32.1 us
    scatter-add x3, other arithmetic, local(): pending[ancestor] = summed.at[row_list(level_no, ancestor)].add(-contrib)  19.5 us
    all_to_all x1, blocking collectives, lane_shape(): lax.all_to_all(jnp.tile(obj, kept_rows), comm_axis, split_axis=at_axis, c...  17.9 us
    ppermute x6, waiting for transfers between devices, from_partner(): lax.ppermute(shard, axis, [(i, i ^ 1 << distance) for i in range(lax.axis...  13.7 us
    all_to_all x3, starting transfers between devices, lane_shape(): lax.all_to_all(jnp.tile(obj, kept_rows), comm_axis, split_axis=at_axis, c...  12 us
  transfers between devices with their start and end apart: 14, of which 14 were waited for; matrix products, arithmetic and copies ran while one was open for 2% of the time, Pallas kernels for 0%

profile of v1, /device:TPU:0, one launch (start us, length us, event | category | flops | bytes accessed | tf_op | source)
XLA Modules:
  0.0 554.1 jit_solution(16046602430832353088)
XLA Ops:
  6.5 1.0 slice.135
  7.6 33.0 %all-gather = bf16[1,1,2048,128]{3,2,1,0:T(8,128)(2,1)S(1)} all-gather(bf16[1,1,256,128]{3,2,1,0:T(8,128)(2,1)S(1)} %slice.135), channel_id=2, replica_groups=mesh['leaf'=4,'blk'=8] {'blk'}, dimensions={2}, use_global_device_ids=true | all-gather | bytes 589824 | tf_op jit(solution)/shard_map/all_gather | solution.py:83
  40.6 1.7 fusion.8
  43.6 6.3 %scatter_custom_fusion = f32[2048,128]{1,0:T(8,128)S(1)} fusion(s32[1024]{0:T(1024)S(1)} %bitcast.151, f32[1024,128]{1,0:T(8,128)S(1)} %copy.31, f32[]{:T(128)} %constant.56.clone.1), kind=kCustom, calls=%fused_computation.38 | custom fusion | flops 131072 | bytes 1048580 | tf_op jit(solution)/shard_map/scatter-add | solution.py:111
  50.8 1.0 copy-done.1
  52.4 79.0 %all-reduce.7.cloned.1.call-done = f32[2,8,128,128]{3,2,1,0:T(8,128)} async-done(((f32[2,8,128,128]{3,2,1,0:T(8,128)}), f32[2,8,128,128]{3,2,1,0:T(8,128)}) %all-reduce.7.cloned.1.call-update) | async-done | bytes 1048592
  131.4 1.5 constant_dynamic-slice_fusion.4
  133.0 1.3 collective-permute-done
  134.4 1.5 fusion.57
  136.8 4.2 all-to-all-start
  141.3 1.0 copy.33
  142.3 6.8 %scatter_custom_fusion.1 = f32[2048,128]{1,0:T(8,128)S(1)} fusion(s32[1024]{0:T(1024)S(1)} %bitcast.150, f32[1024,128]{1,0:T(8,128)} %copy.33, f32[]{:T(128)} %constant.56.clone.1), kind=kCustom, calls=%fused_computation.36 | custom fusion | flops 131072 | bytes 1049088 | tf_op jit(solution)/shard_map/scatter-add | solution.py:111
  149.1 6.7 %all-to-all-done = bf16[2,8,128,128]{3,2,0,1:T(8,128)(2,1)S(1)} async-done(((bf16[2,8,128,128]{3,2,0,1:T(8,128)(2,1)}), bf16[2,8,128,128]{3,2,0,1:T(8,128)(2,1)S(1)}, u32[]{:S(2)}, u32[]{:S(2)}) %all-to-all-start) | async-done | bytes 524320 | tf_op jit(solution)/shard_map/all_to_all | solution.py:24
  156.2 2.0 fusion
  158.2 1.2 copy.34
  159.4 6.4 %scatter_fusion = f32[2048,128]{1,0:T(8,128)S(1)} fusion(f32[2048,128]{1,0:T(8,128)S(1)} %scatter_custom_fusion.1, s32[1024]{0:T(1024)S(1)} %bitcast.149, f32[1024,128]{1,0:T(8,128)S(1)} %copy.34), kind=kCustom, calls=%fused_computation.5 | custom fusion | flops 131072 | bytes 1576960 | tf_op jit(solution)/shard_map/scatter-add | solution.py:111
  166.6 1.0 copy-done
  167.7 77.4 %all-reduce.9.cloned.1.call-done = f32[4,8,64,128]{3,2,1,0:T(8,128)} async-done(((f32[4,8,64,128]{3,2,1,0:T(8,128)}), f32[4,8,64,128]{3,2,1,0:T(8,128)}) %all-reduce.9.cloned.1.call-update) | async-done | bytes 1048592
  245.1 1.5 constant_dynamic-slice_fusion.3
  246.7 1.3 collective-permute-done.1
  248.0 1.5 fusion.75
  249.5 1.5 collective-permute-start.2
  251.1 4.1 collective-permute-done.2
  255.3 17.9 %all_to_all.20 = bf16[4,8,64,128]{3,2,0,1:T(8,128)(2,1)S(1)} all-to-all(bf16[4,8,64,128]{3,2,0,1:T(8,128)(2,1)S(1)} %tile.19), channel_id=1, replica_groups=mesh['leaf'=4,'blk'=8] {'blk'}, dimensions={1} | all-to-all | bytes 1048576 | tf_op jit(solution)/shard_map/all_to_all | solution.py:24
  273.8 1.3 copy.36
  275.2 77.5 %all-reduce.11.cloned.1.call-done = f32[4,8,64,128]{3,2,1,0:T(8,128)} async-done(((f32[4,8,64,128]{3,2,1,0:T(8,128)}), f32[4,8,64,128]{3,2,1,0:T(8,128)}) %all-reduce.11.cloned.1.call-update) | async-done | bytes 1048592
  352.7 1.5 dynamic-slice_bitcast_fusion
  354.3 1.3 collective-permute-done.3
  355.6 1.5 fusion.74
  357.1 1.5 collective-permute-start.4
  358.7 4.1 collective-permute-done.4
  363.7 4.2 all-to-all-start.2
  368.0 13.9 %all-to-all-done.2 = bf16[4,8,64,128]{3,2,0,1:T(8,128)(2,1)S(1)} async-done(((bf16[4,8,64,128]{3,2,0,1:T(8,128)(2,1)}), bf16[4,8,64,128]{3,2,0,1:T(8,128)(2,1)S(1)}, u32[]{:S(2)}, u32[]{:S(2)}) %all-to-all-start.2) | async-done | bytes 524320 | tf_op jit(solution)/shard_map/all_to_all | solution.py:24
  381.9 3.2 gather_fusion
  385.1 2.0 convolution_bitcast_fusion.2
  387.3 1.4 copy.40
  388.8 63.4 %reduce-scatter.12.cloned.1.call-done = f32[2,1,128,128]{3,2,0,1:T(8,128)} async-done(((f32[2,8,128,128]{3,2,0,1:T(8,128)}), f32[2,1,128,128]{3,2,0,1:T(8,128)}) %reduce-scatter.12.cloned.1.call-update) | async-done | bytes 131088 | tf_op jit(solution)/shard_map/reduce_scatter | solution.py:15
  452.1 1.6 collective-permute-done.5
  453.7 0.9 convert_bitcast_fusion
  455.5 3.6 all-to-all-start.3
  459.2 3.2 gather_fusion.2
  462.5 11.5 %all-to-all-done.3 = bf16[2,8,128,128]{3,2,0,1:T(8,128)(2,1)S(1)} async-done(((bf16[2,8,128,128]{3,2,0,1:T(8,128)(2,1)}), bf16[2,8,128,128]{3,2,0,1:T(8,128)(2,1)S(1)}, u32[]{:S(2)}, u32[]{:S(2)}) %all-to-all-start.3) | async-done | bytes 524320 | tf_op jit(solution)/shard_map/all_to_all | solution.py:24
  474.1 3.2 gather_fusion.1
  477.3 2.1 fusion.4
  479.4 1.8 convolution_bitcast_fusion
  481.2 1.3 copy.47
  482.6 63.3 %reduce-scatter.14.cloned.1.call-done = f32[1,1,256,128]{3,2,1,0:T(8,128)} async-done(((f32[1,8,256,128]{3,2,1,0:T(8,128)}), f32[1,1,256,128]{3,2,1,0:T(8,128)}) %reduce-scatter.14.cloned.1.call-update) | async-done | bytes 131088 | tf_op jit(solution)/shard_map/reduce_scatter | solution.py:15
  545.9 1.6 maximum_bitcast_fusion
  (56 shorter events, 8.4 us)
Async XLA Ops:
  6.5 124.9 %all-reduce.7.cloned.1.call-start = ((), (), s32[]{:S(2)}) async-start(), calls=%async_computation.8 | async-start | bytes 2097152
  6.5 35.7 %copy-start.4 = (bf16[1,1,640,1024]{3,2,1,0:T(8,128)(2,1)S(1)}, bf16[1,1,640,1024]{3,2,1,0:T(8,128)(2,1)}, u32[]{:S(2)}) copy-start(bf16[1,1,640,1024]{3,2,1,0:T(8,128)(2,1)} %param.8) | copy-start | bytes 3932164
  42.2 98.8 %copy-start.5 = (f32[256,128]{1,0:T(8,128)}, f32[256,128]{1,0:T(8,128)S(1)}, u32[]{:S(2)}) copy-start(f32[256,128]{1,0:T(8,128)S(1)} %fusion.8) | copy-start | bytes 393220
  42.7 9.1 %copy-start.7 = (u32[32]{0:T(128)S(1)}, u32[32]{0:T(128)}, u32[]{:S(2)}) copy-start(u32[32]{0:T(128)} %constant.76) | copy-start | bytes 388
  50.8 1.0 copy-start.1
  132.9 1.4 collective-permute-start
  136.8 19.0 %all-to-all-start = ((bf16[2,8,128,128]{3,2,0,1:T(8,128)(2,1)}), bf16[2,8,128,128]{3,2,0,1:T(8,128)(2,1)S(1)}, u32[]{:S(2)}, u32[]{:S(2)}) async-start(bf16[2,8,128,128]{3,2,0,1:T(8,128)(2,1)} %tile.17), calls=%async_computation | async-start | bytes 1048576 | tf_op jit(solution)/shard_map/all_to_all | solution.py:24
  141.0 104.1 %all-reduce.9.cloned.1.call-start = ((), (), s32[]{:S(2)}) async-start(), calls=%async_computation.9 | async-start | bytes 2097152
  142.3 13.5 %copy-start.2 = (bf16[1,1,448,2048]{3,2,1,0:T(8,128)(2,1)S(1)}, bf16[1,1,448,2048]{3,2,1,0:T(8,128)(2,1)}, u32[]{:S(2)}) copy-start(bf16[1,1,448,2048]{3,2,1,0:T(8,128)(2,1)} %param.7) | copy-start | bytes 5505028
  166.6 1.0 copy-start
  167.6 185.0 %all-reduce.11.cloned.1.call-start = ((), (), s32[]{:S(2)}) async-start(), calls=%async_computation.10 | async-start | bytes 2097152
  246.6 1.4 collective-permute-start.1
  249.5 5.6 %collective-permute-start.2 = (f32[4,1,64,128]{3,2,1,0:T(8,128)S(1)}, f32[4,1,64,128]{3,2,1,0:T(8,128)S(1)}, u32[]{:S(2)}, u32[]{:S(2)}) collective-permute-start(f32[4,1,64,128]{3,2,1,0:T(8,128)S(1)} %fusion.75), channel_id=1, source_target_pairs={{0,16},{8,24},{16,0},{24,8},{1,17},{9,25},{17,1},{25,9},{2,18},{10... | collective-permute-start | bytes 393224 | tf_op jit(solution)/shard_map/ppermute | solution.py:8
  354.2 1.4 collective-permute-start.3
  357.1 5.6 %collective-permute-start.4 = (f32[4,1,64,128]{3,2,0,1:T(8,128)S(1)}, f32[4,1,64,128]{3,2,0,1:T(8,128)S(1)}, u32[]{:S(2)}, u32[]{:S(2)}) collective-permute-start(f32[4,1,64,128]{3,2,0,1:T(8,128)S(1)} %fusion.74), channel_id=1, source_target_pairs={{0,16},{8,24},{16,0},{24,8},{1,17},{9,25},{17,1},{25,9},{2,18},{10... | collective-permute-start | bytes 393224 | tf_op jit(solution)/shard_map/ppermute | solution.py:8
  363.7 18.2 %all-to-all-start.2 = ((bf16[4,8,64,128]{3,2,0,1:T(8,128)(2,1)}), bf16[4,8,64,128]{3,2,0,1:T(8,128)(2,1)S(1)}, u32[]{:S(2)}, u32[]{:S(2)}) async-start(bf16[4,8,64,128]{3,2,0,1:T(8,128)(2,1)} %tile.41), calls=%async_computation.2 | async-start | bytes 1048576 | tf_op jit(solution)/shard_map/all_to_all | solution.py:24
  367.9 84.2 %reduce-scatter.12.cloned.1.call-start = ((), (), s32[]{:S(2)}) async-start(), calls=%async_computation.6 | async-start | bytes 1179648 | tf_op jit(solution)/shard_map/reduce_scatter | solution.py:15
  452.1 1.6 collective-permute-start.5
  455.5 18.5 %all-to-all-start.3 = ((bf16[2,8,128,128]{3,2,0,1:T(8,128)(2,1)}), bf16[2,8,128,128]{3,2,0,1:T(8,128)(2,1)S(1)}, u32[]{:S(2)}, u32[]{:S(2)}) async-start(bf16[2,8,128,128]{3,2,0,1:T(8,128)(2,1)} %tile.43), calls=%async_computation.4 | async-start | bytes 1048576 | tf_op jit(solution)/shard_map/all_to_all | solution.py:24
  459.1 86.8 %reduce-scatter.14.cloned.1.call-start = ((), (), s32[]{:S(2)}) async-start(), calls=%async_computation.7 | async-start | bytes 1179648 | tf_op jit(solution)/shard_map/reduce_scatter | solution.py:15
  474.1 3.2 copy-start.6
  474.1 5.4 copy-start.3
Sparse Core Ops, SparseCore 0:
  51.9 79.4 all-reduce.6
  167.7 77.2 all-reduce.8
  275.3 77.3 all-reduce.10
  388.9 63.2 reduce-scatter.11
  482.7 63.2 reduce-scatter.13
